TPU v7x, 128 devices: a whole 4x4x4 slice. The times are simulated.
128 devices in a mesh: leaf: 16 (over x_lo, y, core), grid: 8 (over x_hi, z).
Axes of the slice: x: 4 (x_hi: 2, x_lo: 2; x = x_hi * 2 + x_lo), y: 4, z: 4, core: 2. Of those that a mesh axis runs over, the one named last changes fastest.
Arguments:
- child_front: float32 [16, 1, 2048, 2, 8, 128], P('leaf', None, None, None, 'grid'), as said below
- child_live: int32 [16, 1, 16], replicated, may hold values 0 or 1
- child_map: int32 [16, 1, 8], replicated, may hold values from 0 to 15, as said below
- parent_owner: int32 [8, 16], replicated, may hold values from 0 to 15, as said below
- parent_shift: float32 [16, 1, 1, 8, 128], P('leaf', None, None, 'grid'), may hold values from 0.5 to 2
Outputs:
- child_factor: float32 [16, 1, 2048, 1, 8, 128], P('leaf', None, None, None, 'grid')
- parent_done: float32 [16, 1, 2048, 1, 8, 128], P('leaf', None, None, None, 'grid')
Inputs may be any that keep to these rules, and one draw needn't show every extreme that they name: `child_map`: each row holds 8 different block numbers in increasing order, the last one being 15. `parent_owner`: each row is a permutation of the 16 slots. `child_front`: each front is symmetric positive definite.
All inputs are finite; a program needn't handle non-finite values.
Results may differ from a plain program's by a relative error of at most 0.0003.
Values sent between devices are 32-bit elements; how exact they have to be, the bound alone decides.
No kernel may reach another device: no remote copies, remote signals or barrier semaphores. Data moves between devices by JAX's collectives and lax.ppermute only.
A program may use at most 128 MiB of HBM per device.

v0:
```python
import jax
import jax.numpy as jnp
from jax import lax
from jax.sharding import PartitionSpec as P

F = 2048
PIVOTS = 1024
NB = 128
CORDER = 1024
FB = 16
PB = 8
CB = 8


highest = lax.Precision.HIGHEST


def broadcast(value, axis, root):
    mine = lax.axis_index(axis) == root
    return lax.psum(jnp.where(mine, value, jnp.zeros_like(value)), axis)


def swapped_2(value, axis, distance):
    mask = 2**distance
    pairs = [(source, source ^ mask) for source in range(lax.axis_size(axis))]
    return lax.ppermute(value, axis, pairs)


def panel_factor(column_tail):
    lower_part = jnp.linalg.cholesky(column_tail[:, :NB])
    below_part = lax.linalg.triangular_solve(
        lower_part, column_tail[:, NB:], left_side=False, lower=True, transpose_a=True
    )
    return jnp.concatenate([lower_part, below_part], axis=1)


def apply_panel(front_cols, panel_cols, block_ids, panel):
    first_row = panel * NB
    pieces = []
    for round_pick in range(front_cols.shape[2]):
        target = block_ids[round_pick]
        offset = jnp.clip(target * NB - first_row, 0, F - first_row - NB)
        partner = lax.dynamic_slice_in_dim(panel_cols, offset, NB, 1)
        change = jnp.einsum("frn,fsn->frs", panel_cols, partner, precision=highest)
        current = front_cols[:, first_row:, round_pick, :]
        updated = jnp.where(target > panel, current - change, current)
        updated = jnp.where(target == panel, panel_cols, updated)
        upper_rows = jnp.where(target == panel, 0.0, front_cols[:, :first_row, round_pick, :])
        pieces.append(jnp.concatenate([upper_rows, updated], axis=1))
    return jnp.stack(pieces, axis=2)


def mask_front(front_cols, alive_mask, block_ids):
    live_rows = jnp.repeat(alive_mask, NB, axis=1)
    choose = (jnp.arange(FB)[:, None] == block_ids[None, :]).astype(jnp.float32)
    live_cols = jnp.dot(alive_mask, choose, precision=highest)
    places = block_ids[:, None] * NB + jnp.arange(NB)[None, :]
    diagonal = (jnp.arange(F)[:, None, None] == places[None]).astype(jnp.float32)
    kept = front_cols * live_rows[:, :, None, None] * live_cols[:, None, :, None]
    return kept + diagonal[None] * (1.0 - live_cols)[:, None, :, None]


def place_column(schur, targets, alive_mask, target):
    fronts = schur.shape[0]
    pick = (targets == target).astype(jnp.float32) * alive_mask
    tiles = schur.reshape(fronts, CORDER, CB, NB)
    column = jnp.einsum("fc,frcj->frj", pick, tiles, precision=highest)
    spread = (targets[:, None, :] == jnp.arange(FB)[None, :, None]).astype(
        jnp.float32
    ) * alive_mask[:, None, :]
    placed = jnp.einsum(
        "fbc,fcij->fbij", spread, column.reshape(fronts, CB, NB, NB), precision=highest
    )
    return placed.reshape(fronts, F, NB)


def body(child_front, child_live, child_map, parent_owner, parent_shift):
    grid_count = lax.axis_size("grid")
    grid_pos = lax.axis_index("grid")
    leaf_pos = lax.axis_index("leaf")
    member = leaf_pos % 2
    pair = leaf_pos // 2
    sibling = leaf_pos ^ 1
    fronts = child_front.shape[1]
    child_rounds = child_front.shape[3]
    pivot_rounds = PIVOTS // (NB * grid_count)
    parent_rounds = parent_shift.shape[2]
    my_alive = lax.dynamic_index_in_dim(child_live, leaf_pos, 0, keepdims=False).astype(jnp.float32)
    other_alive = lax.dynamic_index_in_dim(child_live, sibling, 0, keepdims=False).astype(
        jnp.float32
    )
    my_map = lax.dynamic_index_in_dim(child_map, leaf_pos, 0, keepdims=False)
    other_map = lax.dynamic_index_in_dim(child_map, sibling, 0, keepdims=False)
    child_blocks = jnp.arange(child_rounds) * grid_count + grid_pos
    front_cols = mask_front(
        child_front.reshape(fronts, F, child_rounds, NB), my_alive, child_blocks
    )
    for panel in range(PB):
        column = front_cols[:, :, panel // grid_count, :]
        outgoing = column
        arrived = broadcast(outgoing, "grid", panel % grid_count)
        column_tail = arrived[:, panel * NB :]
        front_cols = apply_panel(front_cols, panel_factor(column_tail), child_blocks, panel)
    child_factor = front_cols[:, :, :pivot_rounds, :]
    contrib = front_cols[:, PIVOTS:, pivot_rounds:, :]
    gathered = lax.all_gather(contrib[:, :, :, None, :], "grid", axis=3, tiled=True)
    mine_schur = gathered.reshape(fronts, CORDER, CORDER)
    other_schur = swapped_2(mine_schur, "leaf", 0)
    owner_row = lax.dynamic_index_in_dim(parent_owner, pair, 0, keepdims=False)
    slot_ids = (member * grid_count + grid_pos) * parent_rounds + jnp.arange(parent_rounds)
    holders = (owner_row[:, None] == slot_ids[None, :]).astype(jnp.int32)
    parent_blocks = jnp.sum(holders * jnp.arange(FB)[:, None], axis=0)
    shift_cols = parent_shift.reshape(fronts, parent_rounds, NB)
    my_live_contrib = my_alive[:, PB:]
    other_live_contrib = other_alive[:, PB:]
    target = parent_blocks[0]
    column = place_column(mine_schur, my_map, my_live_contrib, target)
    column = column + place_column(other_schur, other_map, other_live_contrib, target)
    places = target * NB + jnp.arange(NB)
    diagonal = (jnp.arange(F)[:, None] == places[None, :]).astype(jnp.float32)
    pieces = [column + diagonal[None] * shift_cols[:, 0, None, :]]
    parent_cols = jnp.stack(pieces, axis=2)
    for panel in range(PB):
        holder = owner_row[panel]
        holder_side = holder // (grid_count * parent_rounds)
        holder_grid = holder // parent_rounds % grid_count
        holder_round = holder % parent_rounds
        column = lax.dynamic_index_in_dim(parent_cols, holder_round, 2, keepdims=False)
        outgoing = column
        arrived = broadcast(outgoing, "grid", holder_grid)
        swapped = swapped_2(arrived, "leaf", 0)
        received = jnp.where(member == holder_side, arrived, swapped)
        column_tail = received[:, panel * NB :]
        parent_cols = apply_panel(parent_cols, panel_factor(column_tail), parent_blocks, panel)
    upper_part = (jnp.arange(F) < PIVOTS)[None, :, None, None] & (parent_blocks >= PB)[
        None, None, :, None
    ]
    parent_cols = jnp.where(upper_part, 0.0, parent_cols)
    return (
        child_factor.reshape(1, fronts, F, pivot_rounds, 1, NB),
        parent_cols.reshape(1, fronts, F, parent_rounds, 1, NB),
    )


def solution(mesh):
    in_specs = (
        P("leaf", None, None, None, "grid", None),
        P(),
        P(),
        P(),
        P("leaf", None, None, "grid", None),
    )
    out_specs = (
        P("leaf", None, None, None, "grid", None),
        P("leaf", None, None, None, "grid", None),
    )
    return jax.shard_map(body, mesh=mesh, in_specs=in_specs, out_specs=out_specs, check_vma=False)
```

profile of v0, /device:TPU:13, one launch (start us, length us, event | category | flops | bytes accessed | tf_op | source)
XLA Modules:
  0.0 2006.0 jit_solution(2481067446718470726)
XLA Ops:
  19.1 79.9 %all-reduce.17.cloned.1.call-done = f32[1,2048,128]{1,2,0:T(8,128)} async-done(((f32[1,2048,128]{1,2,0:T(8,128)}), f32[1,2048,128]{1,2,0:T(8,128)}) %all-reduce.17.cloned.1.call-update) | async-done | bytes 1048592 | tf_op jit(solution)/shard_map/psum | solution.py:20
  100.8 11.7 custom-call.50
  131.1 84.5 %all-reduce.19.cloned.1.call-done = f32[1,2048,128]{1,2,0:T(8,128)} async-done(((f32[1,2048,128]{1,2,0:T(8,128)}), f32[1,2048,128]{1,2,0:T(8,128)}) %all-reduce.19.cloned.1.call-update) | async-done | bytes 1048592 | tf_op jit(solution)/shard_map/psum | solution.py:20
  217.5 11.7 custom-call.52
  246.8 84.3 %all-reduce.21.cloned.1.call-done = f32[1,2048,128]{1,2,0:T(8,128)} async-done(((f32[1,2048,128]{1,2,0:T(8,128)}), f32[1,2048,128]{1,2,0:T(8,128)}) %all-reduce.21.cloned.1.call-update) | async-done | bytes 1048592 | tf_op jit(solution)/shard_map/psum | solution.py:20
  332.9 11.7 custom-call.54
  382.1 64.7 %all-reduce.23.cloned.1.call-done = f32[1,2048,128]{1,2,0:T(8,128)} async-done(((f32[1,2048,128]{1,2,0:T(8,128)}), f32[1,2048,128]{1,2,0:T(8,128)}) %all-reduce.23.cloned.1.call-update) | async-done | bytes 1048592 | tf_op jit(solution)/shard_map/psum | solution.py:20
  448.6 11.7 custom-call.56
  480.0 82.4 %all-reduce.25.cloned.1.call-done = f32[1,2048,128]{1,2,0:T(8,128)} async-done(((f32[1,2048,128]{1,2,0:T(8,128)}), f32[1,2048,128]{1,2,0:T(8,128)}) %all-reduce.25.cloned.1.call-update) | async-done | bytes 1048592 | tf_op jit(solution)/shard_map/psum | solution.py:20
  564.2 11.7 custom-call.58
  596.0 82.9 %all-reduce.27.cloned.1.call-done = f32[1,2048,128]{1,2,0:T(8,128)} async-done(((f32[1,2048,128]{1,2,0:T(8,128)}), f32[1,2048,128]{1,2,0:T(8,128)}) %all-reduce.27.cloned.1.call-update) | async-done | bytes 1048592 | tf_op jit(solution)/shard_map/psum | solution.py:20
  680.7 11.7 custom-call.60
  711.1 82.7 %all-reduce.29.cloned.1.call-done = f32[1,2048,128]{1,2,0:T(8,128)} async-done(((f32[1,2048,128]{1,2,0:T(8,128)}), f32[1,2048,128]{1,2,0:T(8,128)}) %all-reduce.29.cloned.1.call-update) | async-done | bytes 1048592 | tf_op jit(solution)/shard_map/psum | solution.py:20
  795.6 11.7 custom-call.62
  824.2 84.6 %all-reduce.31.cloned.1.call-done = f32[1,2048,128]{1,2,0:T(8,128)} async-done(((f32[1,2048,128]{1,2,0:T(8,128)}), f32[1,2048,128]{1,2,0:T(8,128)}) %all-reduce.31.cloned.1.call-update) | async-done | bytes 1048592 | tf_op jit(solution)/shard_map/psum | solution.py:20
  910.7 11.7 custom-call.64
  937.5 74.7 %all-gather.3.cloned.1.call-done = f32[1,1024,8,128]{3,1,0,2:T(8,128)} async-done(((f32[1,1024,1,128]{3,1,0,2:T(8,128)}), f32[1,1024,8,128]{3,1,0,2:T(8,128)}) %all-gather.3.cloned.1.call-update) | async-done | bytes 4194320 | tf_op jit(solution)/shard_map/all_gather | solution.py:106
  1051.2 79.8 %all-reduce.33.cloned.1.call-done = f32[1,2048,128]{1,2,0:T(8,128)} async-done(((f32[1,2048,128]{1,2,0:T(8,128)}), f32[1,2048,128]{1,2,0:T(8,128)}) %all-reduce.33.cloned.1.call-update) | async-done | bytes 1048592 | tf_op jit(solution)/shard_map/psum | solution.py:20
  1142.7 11.7 custom-call.66
  1169.5 80.0 %all-reduce.35.cloned.1.call-done = f32[1,2048,128]{1,2,0:T(8,128)} async-done(((f32[1,2048,128]{1,2,0:T(8,128)}), f32[1,2048,128]{1,2,0:T(8,128)}) %all-reduce.35.cloned.1.call-update) | async-done | bytes 1048592 | tf_op jit(solution)/shard_map/psum | solution.py:20
  1261.4 11.7 custom-call.68
  1287.9 80.0 %all-reduce.37.cloned.1.call-done = f32[1,2048,128]{1,2,0:T(8,128)} async-done(((f32[1,2048,128]{1,2,0:T(8,128)}), f32[1,2048,128]{1,2,0:T(8,128)}) %all-reduce.37.cloned.1.call-update) | async-done | bytes 1048592 | tf_op jit(solution)/shard_map/psum | solution.py:20
  1379.5 11.7 custom-call.70
  1405.9 80.0 %all-reduce.39.cloned.1.call-done = f32[1,2048,128]{1,2,0:T(8,128)} async-done(((f32[1,2048,128]{1,2,0:T(8,128)}), f32[1,2048,128]{1,2,0:T(8,128)}) %all-reduce.39.cloned.1.call-update) | async-done | bytes 1048592 | tf_op jit(solution)/shard_map/psum | solution.py:20
  1497.8 11.7 custom-call.72
  1524.1 80.0 %all-reduce.41.cloned.1.call-done = f32[1,2048,128]{1,2,0:T(8,128)} async-done(((f32[1,2048,128]{1,2,0:T(8,128)}), f32[1,2048,128]{1,2,0:T(8,128)}) %all-reduce.41.cloned.1.call-update) | async-done | bytes 1048592 | tf_op jit(solution)/shard_map/psum | solution.py:20
  1615.8 11.7 custom-call.74
  1642.0 80.0 %all-reduce.43.cloned.1.call-done = f32[1,2048,128]{1,2,0:T(8,128)} async-done(((f32[1,2048,128]{1,2,0:T(8,128)}), f32[1,2048,128]{1,2,0:T(8,128)}) %all-reduce.43.cloned.1.call-update) | async-done | bytes 1048592 | tf_op jit(solution)/shard_map/psum | solution.py:20
  1733.9 11.7 custom-call.76
  1760.0 80.0 %all-reduce.45.cloned.1.call-done = f32[1,2048,128]{1,2,0:T(8,128)} async-done(((f32[1,2048,128]{1,2,0:T(8,128)}), f32[1,2048,128]{1,2,0:T(8,128)}) %all-reduce.45.cloned.1.call-update) | async-done | bytes 1048592 | tf_op jit(solution)/shard_map/psum | solution.py:20
  1851.9 11.7 custom-call.78
  1877.8 80.0 %all-reduce.47.cloned.1.call-done = f32[1,2048,128]{1,2,0:T(8,128)} async-done(((f32[1,2048,128]{1,2,0:T(8,128)}), f32[1,2048,128]{1,2,0:T(8,128)}) %all-reduce.47.cloned.1.call-update) | async-done | bytes 1048592 | tf_op jit(solution)/shard_map/psum | solution.py:20
  (337 shorter events, 400.2 us)
Async XLA Ops:
  7.2 91.9 %all-reduce.17.cloned.1.call-start = ((), (), s32[]{:S(2)}) async-start(), calls=%async_computation | async-start | bytes 2097152 | tf_op jit(solution)/shard_map/psum | solution.py:20
  16.6 199.1 %all-reduce.19.cloned.1.call-start = ((), (), s32[]{:S(2)}) async-start(), calls=%async_computation.1 | async-start | bytes 2097152 | tf_op jit(solution)/shard_map/psum | solution.py:20
  129.6 201.4 %all-reduce.21.cloned.1.call-start = ((), (), s32[]{:S(2)}) async-start(), calls=%async_computation.2 | async-start | bytes 2097152 | tf_op jit(solution)/shard_map/psum | solution.py:20
  245.1 101.1 %copy-start.5 = (f32[1,2048,1,128]{1,3,2,0:T(8,128)}, f32[1,2048,1,128]{1,3,2,0:T(8,128)S(1)}, u32[]{:S(2)}) copy-start(f32[1,2048,1,128]{1,3,2,0:T(8,128)S(1)} %get-tuple-element.78) | copy-start | bytes 3145732
  245.1 201.7 %all-reduce.23.cloned.1.call-start = ((), (), s32[]{:S(2)}) async-start(), calls=%async_computation.3 | async-start | bytes 2097152 | tf_op jit(solution)/shard_map/psum | solution.py:20
  356.0 2.1 copy-start.6
  360.8 201.6 %all-reduce.25.cloned.1.call-start = ((), (), s32[]{:S(2)}) async-start(), calls=%async_computation.4 | async-start | bytes 2097152 | tf_op jit(solution)/shard_map/psum | solution.py:20
  381.1 92.7 %copy-start.1 = (f32[1,2048,1,128]{1,3,2,0:T(8,128)S(1)}, f32[1,2048,1,128]{1,3,2,0:T(8,128)}, u32[]{:S(2)}) copy-start(f32[1,2048,1,128]{1,3,2,0:T(8,128)} %get-tuple-element.76) | copy-start | bytes 3145732
  476.4 202.5 %all-reduce.27.cloned.1.call-start = ((), (), s32[]{:S(2)}) async-start(), calls=%async_computation.5 | async-start | bytes 2097152 | tf_op jit(solution)/shard_map/psum | solution.py:20
  592.9 200.9 %all-reduce.29.cloned.1.call-start = ((), (), s32[]{:S(2)}) async-start(), calls=%async_computation.6 | async-start | bytes 2097152 | tf_op jit(solution)/shard_map/psum | solution.py:20
  707.8 201.1 %all-reduce.31.cloned.1.call-start = ((), (), s32[]{:S(2)}) async-start(), calls=%async_computation.7 | async-start | bytes 2097152 | tf_op jit(solution)/shard_map/psum | solution.py:20
  822.9 189.3 %all-gather.3.cloned.1.call-start = ((), (), s32[]{:S(2)}) async-start(), calls=%async_computation.16 | async-start | bytes 4718592 | tf_op jit(solution)/shard_map/all_gather | solution.py:106
  937.4 85.8 %copy-start.7 = (s32[16,1,8]{0,2,1:T(8,128)S(1)}, s32[16,1,8]{0,2,1:T(8,128)}, u32[]{:S(2)}) copy-start(s32[16,1,8]{0,2,1:T(8,128)} %param.24) | copy-start | bytes 1540
  937.5 193.6 %all-reduce.33.cloned.1.call-start = ((), (), s32[]{:S(2)}) async-start(), calls=%async_computation.8 | async-start | bytes 2097152 | tf_op jit(solution)/shard_map/psum | solution.py:20
  1017.5 16.3 collective-permute-start
  1047.9 2.0 copy-start.8
  1051.2 198.3 %all-reduce.35.cloned.1.call-start = ((), (), s32[]{:S(2)}) async-start(), calls=%async_computation.9 | async-start | bytes 2097152 | tf_op jit(solution)/shard_map/psum | solution.py:20
  1131.1 10.1 collective-permute-start.1
  1169.4 198.4 %all-reduce.37.cloned.1.call-start = ((), (), s32[]{:S(2)}) async-start(), calls=%async_computation.10 | async-start | bytes 2097152 | tf_op jit(solution)/shard_map/psum | solution.py:20
  1249.5 10.4 collective-permute-start.2
  1287.8 198.0 %all-reduce.39.cloned.1.call-start = ((), (), s32[]{:S(2)}) async-start(), calls=%async_computation.11 | async-start | bytes 2097152 | tf_op jit(solution)/shard_map/psum | solution.py:20
  1367.9 10.1 collective-permute-start.3
  1405.8 198.3 %all-reduce.41.cloned.1.call-start = ((), (), s32[]{:S(2)}) async-start(), calls=%async_computation.12 | async-start | bytes 2097152 | tf_op jit(solution)/shard_map/psum | solution.py:20
  1485.9 10.4 collective-permute-start.4
  1524.0 197.9 %all-reduce.43.cloned.1.call-start = ((), (), s32[]{:S(2)}) async-start(), calls=%async_computation.13 | async-start | bytes 2097152 | tf_op jit(solution)/shard_map/psum | solution.py:20
  1604.1 10.2 collective-permute-start.5
  1641.9 198.1 %all-reduce.45.cloned.1.call-start = ((), (), s32[]{:S(2)}) async-start(), calls=%async_computation.14 | async-start | bytes 2097152 | tf_op jit(solution)/shard_map/psum | solution.py:20
  1722.0 10.5 collective-permute-start.6
  1760.0 197.9 %all-reduce.47.cloned.1.call-start = ((), (), s32[]{:S(2)}) async-start(), calls=%async_computation.15 | async-start | bytes 2097152 | tf_op jit(solution)/shard_map/psum | solution.py:20
  1840.1 10.4 collective-permute-start.7
  1876.6 91.6 %copy-start.2 = (f32[1,2048,1,128]{1,3,2,0:T(8,128)S(1)}, f32[1,2048,1,128]{1,3,2,0:T(8,128)}, u32[]{:S(2)}) copy-start(f32[1,2048,1,128]{1,3,2,0:T(8,128)} %get-tuple-element.68) | copy-start | bytes 3145732
  1957.9 13.2 collective-permute-start.8
  (3 other events, 4.0 us)
Sparse Core Ops, SparseCore 0:
  16.7 82.2 all-reduce.16
  129.8 85.8 all-reduce.18
  245.2 85.8 all-reduce.20
  360.9 85.8 all-reduce.22
  476.5 85.8 all-reduce.24
  593.0 85.8 all-reduce.26
  707.9 85.8 all-reduce.28
  823.0 85.8 all-reduce.30
  937.6 74.5 all-gather.2
  1051.3 79.6 all-reduce.32
  1169.6 79.8 all-reduce.34
  1288.0 79.8 all-reduce.36
  1405.9 79.8 all-reduce.38
  1524.2 79.8 all-reduce.40
  1642.1 79.8 all-reduce.42
  1760.1 79.9 all-reduce.44
  1877.9 79.8 all-reduce.46
where the time goes:
time: 2020 us; the launch traced here: 2010 us
  waiting for transfers between devices  1360 us (67%)
  other arithmetic  413 us (20%)
  between operations  69.7 us (3%)
  matrix products  69.2 us (3%)
  starting transfers between devices  54.7 us (3%)
  local copies, waits for them, and re-layouts  38.3 us (2%)
    psum x16, waiting for transfers between devices, broadcast(): return lax.psum(jnp.where(mine, value, jnp.zeros_like(value)), axis)  1290 us
    another operation x48, other arithmetic, panel_factor(): lower_part = jnp.linalg.cholesky(column_tail[:, :NB])  199 us
    another operation x32, other arithmetic, panel_factor(): lax.linalg.triangular_solve(lower_part, column_tail[:, NB:], left_side=Fa...  168 us
    all_gather x1, waiting for transfers between devices, body(): lax.all_gather(contrib[:, :, :, None, :], 'grid', axis=3, tiled=True)  74.7 us
    ppermute x9, starting transfers between devices, swapped_2(): return lax.ppermute(value, axis, pairs)  52.2 us
  transfers between devices with their start and end apart: 26, of which 17 were waited for; matrix products, arithmetic and copies ran while one was open for 2% of the time, Pallas kernels for 0%

commit v1 on v0

v1 whole, which is shorter than its diff:
```python
import functools

import jax
import jax.numpy as jnp
from jax import lax
from jax.experimental import pallas as pl
from jax.experimental.pallas import tpu as pltpu
from jax.sharding import PartitionSpec as P

NB = 128
PB = 8
FB = 16
HALF = PB * NB
F = FB * NB
VLIMIT = 56 << 20
f32 = jnp.float32
bf16 = jnp.bfloat16


def iota(shape, axis):
    return lax.broadcasted_iota(jnp.int32, shape, axis)


def split(x):
    high = x.astype(bf16)
    return high, (x - high.astype(f32)).astype(bf16)


def dot_nt(a, b):
    return lax.dot_general(a, b, (((1,), (1,)), ((), ())), preferred_element_type=f32)


def dot3(ah, al, bh, bl):
    return dot_nt(ah, bh) + (dot_nt(ah, bl) + dot_nt(al, bh))


def inverse_factor(block, width):
    groups = [block[8 * i : 8 * i + 8, :] for i in range(16)]
    lane = iota((8, NB), 1)
    sub = iota((8, NB), 0)
    own = width // 8
    for step in range(NB // width):
        first = width * step
        top = first // 8
        inside = (lane >= first) & (lane < first + width)
        spread = {}
        for i in range(top, 16):
            for j in range(width):
                if i < top + own and 8 * (i - top) + 7 < j:
                    continue
                spread[i, j] = jnp.broadcast_to(
                    groups[i][:, first + j : first + j + 1], (8, NB)
                )
        diag = {}
        for a in range(width):
            for b in range(a + 1):
                diag[a, b] = jnp.broadcast_to(
                    spread[top + a // 8, b][a % 8 : a % 8 + 1, :], (8, NB)
                )
        rows = []
        for a in range(width):
            row = jnp.broadcast_to(groups[top + a // 8][a % 8 : a % 8 + 1, :], (8, NB))
            rows.append(jnp.where(lane == first + a, 1.0, jnp.where(inside, 0.0, row)))
        recip = {}
        mult = {}
        for j in range(width):
            recip[j] = 1.0 / diag[j, j]
            for a in range(j + 1, width):
                mult[a, j] = diag[a, j] * recip[j]
            for b in range(j + 1, width):
                for a in range(b, width):
                    diag[a, b] = diag[a, b] - mult[a, j] * diag[b, j]
        solved = []
        for a in range(width):
            row = rows[a]
            for b in range(a):
                row = row - mult[a, b] * solved[b]
            solved.append(row)
        for q in range(own):
            total = None
            for s in range(8):
                a = 8 * q + s
                value = solved[a] * lax.rsqrt(diag[a, a])
                total = value if total is None else jnp.where(sub == s, value, total)
            groups[top + q] = total
        back = [None] * width
        for a in reversed(range(width)):
            row = solved[a] * recip[a]
            for b in range(a + 1, width):
                row = row - mult[b, a] * back[b]
            back[a] = row
        for i in range(top + own, 16):
            row = jnp.where(inside, 0.0, groups[i])
            for b in range(width):
                row = row - spread[i, b] * back[b]
            groups[i] = row
    return groups


def factor_chain(m, lh, ll, xh, xl, blocks):
    lower = iota((NB, NB), 0) >= iota((NB, NB), 1)

    def panel(k):
        lo = k * NB
        xhk = xh[k]
        xlk = xl[k]
        for r in range(k, blocks):
            rows = slice(r * NB, r * NB + NB)
            ch, cl = split(m[rows, lo : lo + NB])
            part = dot3(ch, cl, xhk, xlk)
            if r == k:
                part = jnp.where(lower, part, 0.0)
            m[rows, lo : lo + NB] = part
            ph, plow = split(part)
            lh[rows, lo : lo + NB] = ph
            ll[rows, lo : lo + NB] = plow
        if k + 1 < PB:
            nxt = lo + NB
            bh = lh[nxt : nxt + NB, :nxt]
            bl = ll[nxt : nxt + NB, :nxt]
            for r in range(k + 1, blocks, 2):
                rows = slice(r * NB, min(r + 2, blocks) * NB)
                change = dot3(lh[rows, :nxt], ll[rows, :nxt], bh, bl)
                m[rows, nxt : nxt + NB] = m[rows, nxt : nxt + NB] - change

    def body(k, carry):
        off = pl.multiple_of(k * NB, NB)
        groups = inverse_factor(m[pl.ds(off, NB), pl.ds(off, NB)], 16)
        for i in range(16):
            lane = iota((8, NB), 1)
            sub = iota((8, NB), 0) + 8 * i
            high, low = split(jnp.where(lane <= sub, groups[i], 0.0))
            xh[k, 8 * i : 8 * i + 8, :] = high
            xl[k, 8 * i : 8 * i + 8, :] = low
        for static in range(PB):
            pl.when(k == static)(functools.partial(panel, static))
        return carry

    lax.fori_loop(0, PB, body, 0)


def prepare_kernel(meta, front, shift, first_out, second_out):
    g = meta[0]
    eye = (iota((NB, NB), 0) == iota((NB, NB), 1)).astype(f32)

    def alive(block):
        return meta[2 + block].astype(f32)

    def sym(out, base, col, start):
        here = alive(start + g)
        for s in range(5):
            r = (g + s) % PB
            off = pl.multiple_of((start + r) * NB, NB)
            block = front[pl.ds(off, NB), col * NB : col * NB + NB]
            block = block * (here * alive(start + r))
            if s == 0:
                block = block + eye * (1.0 - here)

            @pl.when(r >= g)
            def _():
                out[base + s * NB : base + s * NB + NB, :] = block

            @pl.when(r < g)
            def _():
                out[base + s * NB : base + s * NB + NB, :] = block.T

    sym(first_out, 0, 0, 0)
    first_out[5 * NB : 5 * NB + 8, :] = jnp.broadcast_to(shift[0:1, :], (8, NB))
    here = alive(g)
    for r in range(PB):
        rows = slice(HALF + r * NB, HALF + r * NB + NB)
        second_out[r * NB : r * NB + NB, :] = front[rows, :NB] * (here * alive(PB + r))
    sym(second_out, HALF, 1, PB)


def place_sym(meta, parts, base, target):
    g = meta[0]
    for k in range(PB):
        h = g ^ k
        for s in range(5):
            r = (h + s) % PB
            row = pl.multiple_of(jnp.maximum(r, h) * NB, NB)
            col = pl.multiple_of(jnp.minimum(r, h) * NB, NB)
            target[pl.ds(row, NB), pl.ds(col, NB)] = parts[k][
                base + s * NB : base + s * NB + NB, :
            ]


def child_first_kernel(meta, *refs):
    parts = refs[:PB]
    lh, ll, xh, xl, column, shifts, m = refs[PB:]
    g = meta[0]
    place_sym(meta, parts, 0, m)
    shifts[...] = jnp.zeros_like(shifts)
    for k in range(PB):
        off = pl.multiple_of((g ^ k) * NB, NB)
        shifts[:, pl.ds(off, NB)] = parts[k][5 * NB : 5 * NB + 8, :]
    lh[...] = jnp.zeros_like(lh)
    ll[...] = jnp.zeros_like(ll)
    factor_chain(m, lh, ll, xh, xl, PB)
    mine = pl.multiple_of(g * NB, NB)
    for r in range(PB):
        block = m[r * NB : r * NB + NB, pl.ds(mine, NB)]
        column[r * NB : r * NB + NB, :] = jnp.where(r >= g, block, 0.0)


def child_second_kernel(meta, lh, ll, xh, xl, column, shifts, *refs):
    parts = refs[:PB]
    factor, schur, m, bh, bl = refs[PB:]
    g = meta[0]
    for k in range(PB):
        off = pl.multiple_of((g ^ k) * NB, NB)
        m[:, pl.ds(off, NB)] = parts[k][:HALF, :]
    place_sym(meta, parts, HALF, schur)
    schur[HALF : HALF + 8, :] = shifts[...]
    for k in range(PB):
        lo = k * NB
        for r in range(0, PB, 2):
            rows = slice(r * NB, r * NB + 2 * NB)
            value = m[rows, lo : lo + NB]
            if k:
                value = value - dot3(
                    bh[rows, :lo], bl[rows, :lo], lh[lo : lo + NB, :lo], ll[lo : lo + NB, :lo]
                )
            ch, cl = split(value)
            part = dot3(ch, cl, xh[k], xl[k])
            m[rows, lo : lo + NB] = part
            ph, plow = split(part)
            bh[rows, lo : lo + NB] = ph
            bl[rows, lo : lo + NB] = plow
    lower = iota((NB, NB), 0) >= iota((NB, NB), 1)
    for c in range(0, PB, 2):
        cols = slice(c * NB, c * NB + 2 * NB)
        for r in range(c, PB, 2):
            rows = slice(r * NB, r * NB + 2 * NB)
            change = dot3(bh[rows, :], bl[rows, :], bh[cols, :], bl[cols, :])
            schur[rows, cols] = schur[rows, cols] - change
    mine = pl.multiple_of(g * NB, NB)
    factor[:HALF, :] = column[...]
    factor[HALF:, :] = m[:, pl.ds(mine, NB)]


def parent_kernel(meta, own, other, out, m, lh, ll, xh, xl, inverse):
    g = meta[0]
    member = meta[1]
    slot = member * PB + g
    for side in range(2):
        for q in range(FB):
            inverse[side, q] = -1
        for c in range(PB):
            live = meta[2 + 16 * side + PB + c]
            dest = meta[34 + 8 * side + c]
            inverse[side, dest] = jnp.where(live > 0, c, -1)
    mine = jnp.int32(0)
    for q in range(FB):
        mine = jnp.where(meta[50 + q] == slot, q, mine)
    sides = (own, other)
    eye = iota((NB, NB), 0) == iota((NB, NB), 1)

    def diagonal(block):
        holder = meta[50 + block]
        off = pl.multiple_of(holder % PB * NB, NB)
        a = own[HALF : HALF + 1, pl.ds(off, NB)]
        b = other[HALF : HALF + 1, pl.ds(off, NB)]
        row = jnp.where(holder // PB == member, a, b)
        return jnp.where(eye, jnp.broadcast_to(row, (NB, NB)), 0.0)

    for p in range(PB):
        for q in range(p, FB):
            where = (slice(q * NB, q * NB + NB), slice(p * NB, p * NB + NB))
            m[where] = diagonal(p) if p == q else jnp.zeros((NB, NB), f32)
            for side in range(2):
                ci = inverse[side, q]
                cj = inverse[side, p]

                @pl.when((ci >= 0) & (cj >= 0))
                def _():
                    ro = pl.multiple_of(ci * NB, NB)
                    co = pl.multiple_of(cj * NB, NB)
                    m[where] = m[where] + sides[side][pl.ds(ro, NB), pl.ds(co, NB)]

    lh[...] = jnp.zeros_like(lh)
    ll[...] = jnp.zeros_like(ll)
    factor_chain(m, lh, ll, xh, xl, FB)

    @pl.when(mine < PB)
    def _():
        off = pl.multiple_of(mine * NB, NB)
        for r in range(FB):
            block = m[r * NB : r * NB + NB, pl.ds(off, NB)]
            out[r * NB : r * NB + NB, :] = jnp.where(r >= mine, block, 0.0)

    @pl.when(mine >= PB)
    def _():
        out[:HALF, :] = jnp.zeros((HALF, NB), f32)
        off = pl.multiple_of(mine * NB, NB)
        rh = lh[pl.ds(off, NB), :]
        rl = ll[pl.ds(off, NB), :]
        diag = diagonal(mine)
        for q in range(PB, FB):
            rows = slice(q * NB, q * NB + NB)
            out[rows, :] = jnp.where(mine == q, diag, 0.0) - dot3(
                lh[rows, :], ll[rows, :], rh, rl
            )
            for side in range(2):
                ci = inverse[side, q]
                cj = inverse[side, mine]
                high = pl.multiple_of(jnp.maximum(jnp.maximum(ci, cj), 0) * NB, NB)
                low = pl.multiple_of(jnp.maximum(jnp.minimum(ci, cj), 0) * NB, NB)

                @pl.when((ci >= cj) & (cj >= 0))
                def _():
                    out[rows, :] = out[rows, :] + sides[side][pl.ds(high, NB), pl.ds(low, NB)]

                @pl.when((ci >= 0) & (ci < cj))
                def _():
                    out[rows, :] = out[rows, :] + sides[side][pl.ds(high, NB), pl.ds(low, NB)].T


VM = pl.BlockSpec(memory_space=pltpu.VMEM)
SM = pl.BlockSpec(memory_space=pltpu.SMEM)


def shape(*dims, dtype=f32):
    return jax.ShapeDtypeStruct(dims, dtype)


def run(kernel, outs, scratch, flops, meta, *args):
    return pl.pallas_call(
        kernel,
        out_shape=outs,
        in_specs=[SM] + [VM] * len(args),
        out_specs=jax.tree.map(lambda _: VM, outs),
        scratch_shapes=scratch,
        compiler_params=pltpu.CompilerParams(vmem_limit_bytes=VLIMIT),
        cost_estimate=pl.CostEstimate(flops=flops, bytes_accessed=1 << 22, transcendentals=0),
    )(meta, *args)


def exchange(value):
    parts = [value]
    for k in range(1, PB):
        parts.append(lax.ppermute(value, "grid", [(s, s ^ k) for s in range(PB)]))
    return parts


def body(child_front, child_live, child_map, parent_owner, parent_shift):
    g = lax.axis_index("grid").astype(jnp.int32)
    leaf = lax.axis_index("leaf").astype(jnp.int32)
    sibling = leaf ^ 1

    def row(table, index):
        return lax.dynamic_index_in_dim(table.reshape(table.shape[0], -1), index, 0, keepdims=False)

    meta = jnp.concatenate(
        [
            jnp.stack([g, leaf % 2]),
            row(child_live, leaf),
            row(child_live, sibling),
            row(child_map, leaf),
            row(child_map, sibling),
            row(parent_owner, leaf // 2),
        ]
    )
    front = child_front.reshape(F, 2 * NB)
    shift = parent_shift.reshape(1, NB)
    first, second = run(
        prepare_kernel,
        (shape(5 * NB + 8, NB), shape(HALF + 5 * NB, NB)),
        [],
        1 << 20,
        meta,
        front,
        shift,
    )
    first_parts = exchange(first)
    first_parts, second = lax.optimization_barrier((first_parts, second))
    second_parts = exchange(second)
    square = shape(HALF, HALF, dtype=bf16)
    lh, ll, xh, xl, column, shifts = run(
        child_first_kernel,
        (
            square,
            square,
            shape(PB, NB, NB, dtype=bf16),
            shape(PB, NB, NB, dtype=bf16),
            shape(HALF, NB),
            shape(8, HALF),
        ),
        [pltpu.VMEM((HALF, HALF), f32)],
        40 * 10**9,
        meta,
        *first_parts,
    )
    factor, schur = run(
        child_second_kernel,
        (shape(F, NB), shape(HALF + 8, HALF)),
        [
            pltpu.VMEM((HALF, HALF), f32),
            pltpu.VMEM((HALF, HALF), bf16),
            pltpu.VMEM((HALF, HALF), bf16),
        ],
        10**10,
        meta,
        lh,
        ll,
        xh,
        xl,
        column,
        shifts,
        *second_parts,
    )
    other = lax.ppermute(schur, "leaf", [(s, s ^ 1) for s in range(lax.axis_size("leaf"))])
    done = run(
        parent_kernel,
        shape(F, NB),
        [
            pltpu.VMEM((F, HALF), f32),
            pltpu.VMEM((F, HALF), bf16),
            pltpu.VMEM((F, HALF), bf16),
            pltpu.VMEM((PB, NB, NB), bf16),
            pltpu.VMEM((PB, NB, NB), bf16),
            pltpu.SMEM((2, FB), jnp.int32),
        ],
        40 * 10**9,
        meta,
        schur,
        other,
    )
    return factor.reshape(1, 1, F, 1, 1, NB), done.reshape(1, 1, F, 1, 1, NB)


def solution(mesh):
    in_specs = (
        P("leaf", None, None, None, "grid", None),
        P(),
        P(),
        P(),
        P("leaf", None, None, "grid", None),
    )
    out_specs = (
        P("leaf", None, None, None, "grid", None),
        P("leaf", None, None, None, "grid", None),
    )
    return jax.shard_map(body, mesh=mesh, in_specs=in_specs, out_specs=out_specs, check_vma=False)
```

time: 2020 us -> 262 us (0.13)
  waiting for transfers between devices: 1360 us -> 69.8 us
  other arithmetic: 413 us -> 0 us
  Pallas kernels: 0 us -> 151 us
  matrix products: 69.2 us -> 0 us
  between operations: 69.7 us -> 1.03 us
  local copies, waits for them, and re-layouts: 38.3 us -> 9.42 us
  starting transfers between devices: 54.7 us -> 26.8 us
    psum x16 -> x0, waiting for transfers between devices: 1290 us -> none  [broadcast(): return lax.psum(jnp.where(mine, value, jnp.zeros_like(value)), axis)]
    another operation x94 -> x0, other arithmetic: 376 us -> none  [the longest x48 199 us: panel_factor(): lower_part = jnp.linalg.cholesky(column_tail[:, :NB])]
    pallas_call x0 -> x4, Pallas kernels: none -> 151 us  [run(): pl.pallas_call(kernel, out_shape=outs, in_specs=[SM] + [VM] * len(args),...]
    all_gather x1 -> x0, waiting for transfers between devices: 74.7 us -> none  [body(): lax.all_gather(contrib[:, :, :, None, :], 'grid', axis=3, tiled=True)]
    ppermute x9 -> x15, waiting for transfers between devices: 0.02 us -> 69.8 us  [the longest x14 62.7 us: exchange(): parts.append(lax.ppermute(value, 'grid', [(s, s ^ k) for s in range(PB)]))]
    dot_general x29 -> x0, matrix products: 47.2 us -> none  [the longest x24 28.9 us: apply_panel(): change = jnp.einsum('frn,fsn->frs', panel_cols, partner, precision=highest)]
    select_n x40 -> x0, other arithmetic: 26.4 us -> none  [the longest x10 13 us: broadcast(): return lax.psum(jnp.where(mine, value, jnp.zeros_like(value)), axis)]
    ppermute x9 -> x15, starting transfers between devices: 52.2 us -> 26.8 us  [the longest x14 24.1 us: exchange(): parts.append(lax.ppermute(value, 'grid', [(s, s ^ k) for s in range(PB)]))]
  transfers between devices with their start and end apart: 26 -> 15, of which waited for: 17 -> 8; matrix products, arithmetic and copies ran while one was open for 2% -> 0% of each run, Pallas kernels for 0% -> 20%
where the time goes in v1:
time: 262 us; the launch traced here: 258 us
  Pallas kernels  151 us (58%)
  waiting for transfers between devices  69.8 us (27%)
  starting transfers between devices  26.8 us (10%)
  local copies, waits for them, and re-layouts  9.42 us (4%)
    pallas_call x4, Pallas kernels, run(): pl.pallas_call(kernel, out_shape=outs, in_specs=[SM] + [VM] * len(args),...  151 us
    ppermute x14, waiting for transfers between devices, exchange(): parts.append(lax.ppermute(value, 'grid', [(s, s ^ k) for s in range(PB)]))  62.7 us
    ppermute x14, starting transfers between devices, exchange(): parts.append(lax.ppermute(value, 'grid', [(s, s ^ k) for s in range(PB)]))  24.1 us
    unnamed x33, local copies, waits for them, and re-layouts  7.15 us
    ppermute x1, waiting for transfers between devices, body(): lax.ppermute(schur, 'leaf', [(s, s ^ 1) for s in range(lax.axis_size('lea...  7.04 us
  transfers between devices with their start and end apart: 15, of which 8 were waited for; matrix products, arithmetic and copies ran while one was open for 0% of the time, Pallas kernels for 20%

profile of v1, /device:TPU:13, one launch (start us, length us, event | category | flops | bytes accessed | tf_op | source)
XLA Modules:
  0.0 257.6 jit_solution(8204620000863003396)
XLA Ops:
  0.7 0.7 fusion.1
  1.4 1.0 dynamic-slice_reduce_fusion
  2.3 3.1 %copy.11 = f32[256,8,2,128]{3,1,2,0:T(8,128)} copy(f32[256,8,2,128]{3,2,1,0:T(2,128)} %bitcast.22) | data formatting | bytes 4194304
  5.4 0.6 concatenate.3.meta
  6.0 3.0 %shard_map.68 = (f32[648,128]{1,0:T(8,128)}, f32[1664,128]{1,0:T(8,128)}) custom-call(s32[66]{0:T(128)} %concatenate.3.meta, f32[2048,256]{1,0:T(8,128)} %bitcast.21, f32[1,128]{1,0:T(1,128)} %bitcast.23), custom_call_target="tpu_custom_call" | custom-call | flops 1048576 | bytes 4194304 | tf_op jit(solution)/shard_map/pallas_call | solution.py:329
  9.1 3.5 %collective-permute-start.6 = (f32[648,128]{1,0:T(8,128)}, f32[648,128]{1,0:T(8,128)S(1)}, u32[]{:S(2)}, u32[]{:S(2)}) collective-permute-start(f32[648,128]{1,0:T(8,128)} %get-tuple-element.23.refs_0_), channel_id=1, source_target_pairs={{0,7},{1,6},{2,5},{3,4},{4,3},{5,2},{6,1},{7,0},{8,15},{9,14},{10,... | collective-permute-start | bytes 995336 | tf_op jit(solution)/shard_map/ppermute | solution.py:343
  12.6 2.5 collective-permute-start.5
  15.1 1.3 collective-permute-start.4
  16.3 1.1 collective-permute-start.3
  17.4 4.3 %collective-permute-start.2 = (f32[648,128]{1,0:T(8,128)}, f32[648,128]{1,0:T(8,128)S(1)}, u32[]{:S(2)}, u32[]{:S(2)}) collective-permute-start(f32[648,128]{1,0:T(8,128)} %get-tuple-element.23.refs_0_), channel_id=1, source_target_pairs={{0,3},{1,2},{2,1},{3,0},{4,7},{5,6},{6,5},{7,4},{8,11},{9,10},{10,... | collective-permute-start | bytes 995336 | tf_op jit(solution)/shard_map/ppermute | solution.py:343
  21.7 2.6 %collective-permute-start.1 = (f32[648,128]{1,0:T(8,128)}, f32[648,128]{1,0:T(8,128)S(1)}, u32[]{:S(2)}, u32[]{:S(2)}) collective-permute-start(f32[648,128]{1,0:T(8,128)} %get-tuple-element.23.refs_0_), channel_id=1, source_target_pairs={{0,2},{1,3},{2,0},{3,1},{4,6},{5,7},{6,4},{7,5},{8,10},{9,11},{10,... | collective-permute-start | bytes 995336 | tf_op jit(solution)/shard_map/ppermute | solution.py:343
  24.3 5.3 %collective-permute-done.5.refs_6_ = f32[648,128]{1,0:T(8,128)S(1)} collective-permute-done((f32[648,128]{1,0:T(8,128)}, f32[648,128]{1,0:T(8,128)S(1)}, u32[]{:S(2)}, u32[]{:S(2)}) %collective-permute-start.5) | collective-permute-done | bytes 331808 | tf_op jit(solution)/shard_map/ppermute | solution.py:343
  29.6 8.1 %collective-permute-done.4.refs_5_ = f32[648,128]{1,0:T(8,128)S(1)} collective-permute-done((f32[648,128]{1,0:T(8,128)}, f32[648,128]{1,0:T(8,128)S(1)}, u32[]{:S(2)}, u32[]{:S(2)}) %collective-permute-start.4) | collective-permute-done | bytes 331808 | tf_op jit(solution)/shard_map/ppermute | solution.py:343
  37.7 7.1 %collective-permute-done.3.refs_4_ = f32[648,128]{1,0:T(8,128)S(1)} collective-permute-done((f32[648,128]{1,0:T(8,128)}, f32[648,128]{1,0:T(8,128)S(1)}, u32[]{:S(2)}, u32[]{:S(2)}) %collective-permute-start.3) | collective-permute-done | bytes 331808 | tf_op jit(solution)/shard_map/ppermute | solution.py:343
  44.8 0.1 collective-permute-done.1.refs_2_
  44.9 8.1 %collective-permute-done.refs_1_ = f32[648,128]{1,0:T(8,128)S(1)} collective-permute-done((f32[648,128]{1,0:T(8,128)}, f32[648,128]{1,0:T(8,128)S(1)}, u32[]{:S(2)}, u32[]{:S(2)}) %collective-permute-start) | collective-permute-done | bytes 331808 | tf_op jit(solution)/shard_map/ppermute | solution.py:343
  53.0 5.3 %collective-permute-start.12 = (f32[1664,128]{1,0:T(8,128)}, f32[1664,128]{1,0:T(8,128)S(1)}, u32[]{:S(2)}, u32[]{:S(2)}) collective-permute-start(f32[1664,128]{1,0:T(8,128)} %get-tuple-element.37.refs_0_), channel_id=1, source_target_pairs={{0,6},{1,7},{2,4},{3,5},{4,2},{5,3},{6,0},{7,1},{8,14},{9,15},{10,... | collective-permute-start | bytes 2555912 | tf_op jit(solution)/shard_map/ppermute | solution.py:343
  58.3 3.0 %collective-permute-start.10 = (f32[1664,128]{1,0:T(8,128)}, f32[1664,128]{1,0:T(8,128)S(1)}, u32[]{:S(2)}, u32[]{:S(2)}) collective-permute-start(f32[1664,128]{1,0:T(8,128)} %get-tuple-element.37.refs_0_), channel_id=1, source_target_pairs={{0,4},{1,5},{2,6},{3,7},{4,0},{5,1},{6,2},{7,3},{8,12},{9,13},{10,... | collective-permute-start | bytes 2555912 | tf_op jit(solution)/shard_map/ppermute | solution.py:343
  61.3 15.5 %collective-permute-done.13.refs_7_ = f32[1664,128]{1,0:T(8,128)S(1)} collective-permute-done((f32[1664,128]{1,0:T(8,128)}, f32[1664,128]{1,0:T(8,128)S(1)}, u32[]{:S(2)}, u32[]{:S(2)}) %collective-permute-start.13) | collective-permute-done | bytes 852000 | tf_op jit(solution)/shard_map/ppermute | solution.py:343
  76.8 18.5 %collective-permute-done.12.refs_6_ = f32[1664,128]{1,0:T(8,128)S(1)} collective-permute-done((f32[1664,128]{1,0:T(8,128)}, f32[1664,128]{1,0:T(8,128)S(1)}, u32[]{:S(2)}, u32[]{:S(2)}) %collective-permute-start.12) | collective-permute-done | bytes 852000 | tf_op jit(solution)/shard_map/ppermute | solution.py:343
  95.4 0.5 collective-permute-start.7
  95.9 52.8 %shard_map.69 = (bf16[1024,1024]{1,0:T(8,128)(2,1)}, bf16[1024,1024]{1,0:T(8,128)(2,1)}, bf16[8,128,128]{2,1,0:T(8,128)(2,1)}, bf16[8,128,128]{2,1,0:T(8,128)(2,...) custom-call(s32[66]{0:T(128)} %concatenate.3.meta, f32[648,128]{1,0:T(8,128)} %get-tuple-element.23.refs_0_, ...), custom_call_target="tpu_custom_call" | custom-call | flops 40000000000 | bytes 4194304 | tf_op jit(solution)/shard_map/pallas_call | solution.py:329
  148.8 0.8 copy-done.4
  149.6 0.3 copy-done.5
  150.0 0.3 copy-done.6
  150.3 0.3 copy-done.7
  150.6 0.2 copy-done.8
  150.8 24.2 %shard_map.70 = (f32[2048,128]{1,0:T(8,128)}, f32[1032,1024]{1,0:T(8,128)}) custom-call(s32[66]{0:T(128)} %concatenate.3.meta, bf16[1024,1024]{1,0:T(8,128)(2,1)} %get-tuple-element.31.lh, bf16[1024,1024]{1,0:T(8,128)(2,1)} %get-tuple-element.32.ll, bf16[8,128,128]{2,1,0:T(8,128)(2,1)} %get-tuple-element.33.xh, bf16[8,128,128]{2,1,0:T(8,128)(2,1)} %get-tuple-element.34.xl, ...), custom_call_target="tpu_custom_call" | custom-call | flops 10000000000 | bytes 4194304 | tf_op jit(solution)/shard_map/pallas_call | solution.py:329
  175.1 2.7 %collective-permute-start.14 = (f32[1032,1024]{1,0:T(8,128)}, f32[1032,1024]{1,0:T(8,128)S(1)}, u32[]{:S(2)}, u32[]{:S(2)}) collective-permute-start(f32[1032,1024]{1,0:T(8,128)} %get-tuple-element.39.own), channel_id=1, source_target_pairs={{0,8},{8,0},{16,24},{24,16},{32,40},{40,32},{48,56},{56,48},{64,72... | collective-permute-start | bytes 12681224 | tf_op jit(solution)/shard_map/ppermute | solution.py:413
  177.7 7.0 %collective-permute-done.14.other = f32[1032,1024]{1,0:T(8,128)S(1)} collective-permute-done((f32[1032,1024]{1,0:T(8,128)}, f32[1032,1024]{1,0:T(8,128)S(1)}, u32[]{:S(2)}, u32[]{:S(2)}) %collective-permute-start.14) | collective-permute-done | bytes 4227104 | tf_op jit(solution)/shard_map/ppermute | solution.py:413
  184.8 2.0 copy-done.1
  186.8 70.6 %shard_map.71 = f32[2048,128]{1,0:T(8,128)} custom-call(s32[66]{0:T(128)} %concatenate.3.meta, f32[1032,1024]{1,0:T(8,128)} %get-tuple-element.39.own, f32[1032,1024]{1,0:T(8,128)} %copy-done.1), custom_call_target="tpu_custom_call" | custom-call | flops 40000000000 | bytes 4194304 | tf_op jit(solution)/shard_map/pallas_call | solution.py:329
  (39 shorter events, 0.1 us)
Async XLA Ops:
  0.6 4.8 %copy-start = (s32[8,16]{1,0:T(8,128)S(1)}, s32[8,16]{1,0:T(8,128)}, u32[]{:S(2)}) copy-start(s32[8,16]{1,0:T(8,128)} %param.8) | copy-start | bytes 1540
  9.1 12.6 %collective-permute-start.6 = (f32[648,128]{1,0:T(8,128)}, f32[648,128]{1,0:T(8,128)S(1)}, u32[]{:S(2)}, u32[]{:S(2)}) collective-permute-start(f32[648,128]{1,0:T(8,128)} %get-tuple-element.23.refs_0_), channel_id=1, source_target_pairs={{0,7},{1,6},{2,5},{3,4},{4,3},{5,2},{6,1},{7,0},{8,15},{9,14},{10,... | collective-permute-start | bytes 995336 | tf_op jit(solution)/shard_map/ppermute | solution.py:343
  12.6 17.0 %collective-permute-start.5 = (f32[648,128]{1,0:T(8,128)}, f32[648,128]{1,0:T(8,128)S(1)}, u32[]{:S(2)}, u32[]{:S(2)}) collective-permute-start(f32[648,128]{1,0:T(8,128)} %get-tuple-element.23.refs_0_), channel_id=1, source_target_pairs={{0,6},{1,7},{2,4},{3,5},{4,2},{5,3},{6,0},{7,1},{8,14},{9,15},{10,... | collective-permute-start | bytes 995336 | tf_op jit(solution)/shard_map/ppermute | solution.py:343
  15.1 22.6 %collective-permute-start.4 = (f32[648,128]{1,0:T(8,128)}, f32[648,128]{1,0:T(8,128)S(1)}, u32[]{:S(2)}, u32[]{:S(2)}) collective-permute-start(f32[648,128]{1,0:T(8,128)} %get-tuple-element.23.refs_0_), channel_id=1, source_target_pairs={{0,5},{1,4},{2,7},{3,6},{4,1},{5,0},{6,3},{7,2},{8,13},{9,12},{10,... | collective-permute-start | bytes 995336 | tf_op jit(solution)/shard_map/ppermute | solution.py:343
  16.3 28.4 %collective-permute-start.3 = (f32[648,128]{1,0:T(8,128)}, f32[648,128]{1,0:T(8,128)S(1)}, u32[]{:S(2)}, u32[]{:S(2)}) collective-permute-start(f32[648,128]{1,0:T(8,128)} %get-tuple-element.23.refs_0_), channel_id=1, source_target_pairs={{0,4},{1,5},{2,6},{3,7},{4,0},{5,1},{6,2},{7,3},{8,12},{9,13},{10,... | collective-permute-start | bytes 995336 | tf_op jit(solution)/shard_map/ppermute | solution.py:343
  17.4 27.4 %collective-permute-start.2 = (f32[648,128]{1,0:T(8,128)}, f32[648,128]{1,0:T(8,128)S(1)}, u32[]{:S(2)}, u32[]{:S(2)}) collective-permute-start(f32[648,128]{1,0:T(8,128)} %get-tuple-element.23.refs_0_), channel_id=1, source_target_pairs={{0,3},{1,2},{2,1},{3,0},{4,7},{5,6},{6,5},{7,4},{8,11},{9,10},{10,... | collective-permute-start | bytes 995336 | tf_op jit(solution)/shard_map/ppermute | solution.py:343
  21.7 74.2 %copy-start.9 = (f32[648,128]{1,0:T(8,128)}, f32[648,128]{1,0:T(8,128)S(1)}, u32[]{:S(2)}) copy-start(f32[648,128]{1,0:T(8,128)S(1)} %collective-permute-done.6.refs_7_) | copy-start | bytes 995332
  21.7 23.2 %collective-permute-start.1 = (f32[648,128]{1,0:T(8,128)}, f32[648,128]{1,0:T(8,128)S(1)}, u32[]{:S(2)}, u32[]{:S(2)}) collective-permute-start(f32[648,128]{1,0:T(8,128)} %get-tuple-element.23.refs_0_), channel_id=1, source_target_pairs={{0,2},{1,3},{2,0},{3,1},{4,6},{5,7},{6,4},{7,5},{8,10},{9,11},{10,... | collective-permute-start | bytes 995336 | tf_op jit(solution)/shard_map/ppermute | solution.py:343
  29.6 66.3 %copy-start.10 = (f32[648,128]{1,0:T(8,128)}, f32[648,128]{1,0:T(8,128)S(1)}, u32[]{:S(2)}) copy-start(f32[648,128]{1,0:T(8,128)S(1)} %collective-permute-done.5.refs_6_) | copy-start | bytes 995332
  29.6 23.4 %collective-permute-start = (f32[648,128]{1,0:T(8,128)}, f32[648,128]{1,0:T(8,128)S(1)}, u32[]{:S(2)}, u32[]{:S(2)}) collective-permute-start(f32[648,128]{1,0:T(8,128)} %get-tuple-element.23.refs_0_), channel_id=1, source_target_pairs={{0,1},{1,0},{2,3},{3,2},{4,5},{5,4},{6,7},{7,6},{8,9},{9,8},{10,11... | collective-permute-start | bytes 995336 | tf_op jit(solution)/shard_map/ppermute | solution.py:343
  37.7 58.2 %copy-start.11 = (f32[648,128]{1,0:T(8,128)}, f32[648,128]{1,0:T(8,128)S(1)}, u32[]{:S(2)}) copy-start(f32[648,128]{1,0:T(8,128)S(1)} %collective-permute-done.4.refs_5_) | copy-start | bytes 995332
  44.8 51.1 %copy-start.12 = (f32[648,128]{1,0:T(8,128)}, f32[648,128]{1,0:T(8,128)S(1)}, u32[]{:S(2)}) copy-start(f32[648,128]{1,0:T(8,128)S(1)} %collective-permute-done.3.refs_4_) | copy-start | bytes 995332
  44.8 51.1 %copy-start.13 = (f32[648,128]{1,0:T(8,128)}, f32[648,128]{1,0:T(8,128)S(1)}, u32[]{:S(2)}) copy-start(f32[648,128]{1,0:T(8,128)S(1)} %collective-permute-done.2.refs_3_) | copy-start | bytes 995332
  44.9 51.0 %copy-start.14 = (f32[648,128]{1,0:T(8,128)}, f32[648,128]{1,0:T(8,128)S(1)}, u32[]{:S(2)}) copy-start(f32[648,128]{1,0:T(8,128)S(1)} %collective-permute-done.1.refs_2_) | copy-start | bytes 995332
  53.0 8.4 %copy-start.15 = (f32[648,128]{1,0:T(8,128)}, f32[648,128]{1,0:T(8,128)S(1)}, u32[]{:S(2)}) copy-start(f32[648,128]{1,0:T(8,128)S(1)} %collective-permute-done.refs_1_) | copy-start | bytes 995332
  53.0 23.8 %collective-permute-start.13 = (f32[1664,128]{1,0:T(8,128)}, f32[1664,128]{1,0:T(8,128)S(1)}, u32[]{:S(2)}, u32[]{:S(2)}) collective-permute-start(f32[1664,128]{1,0:T(8,128)} %get-tuple-element.37.refs_0_), channel_id=1, source_target_pairs={{0,7},{1,6},{2,5},{3,4},{4,3},{5,2},{6,1},{7,0},{8,15},{9,14},{10,... | collective-permute-start | bytes 2555912 | tf_op jit(solution)/shard_map/ppermute | solution.py:343
  53.0 42.4 %collective-permute-start.12 = (f32[1664,128]{1,0:T(8,128)}, f32[1664,128]{1,0:T(8,128)S(1)}, u32[]{:S(2)}, u32[]{:S(2)}) collective-permute-start(f32[1664,128]{1,0:T(8,128)} %get-tuple-element.37.refs_0_), channel_id=1, source_target_pairs={{0,6},{1,7},{2,4},{3,5},{4,2},{5,3},{6,0},{7,1},{8,14},{9,15},{10,... | collective-permute-start | bytes 2555912 | tf_op jit(solution)/shard_map/ppermute | solution.py:343
  58.3 90.4 %collective-permute-start.11 = (f32[1664,128]{1,0:T(8,128)}, f32[1664,128]{1,0:T(8,128)S(1)}, u32[]{:S(2)}, u32[]{:S(2)}) collective-permute-start(f32[1664,128]{1,0:T(8,128)} %get-tuple-element.37.refs_0_), channel_id=1, source_target_pairs={{0,5},{1,4},{2,7},{3,6},{4,1},{5,0},{6,3},{7,2},{8,13},{9,12},{10,... | collective-permute-start | bytes 2555912 | tf_op jit(solution)/shard_map/ppermute | solution.py:343
  58.3 90.4 %collective-permute-start.10 = (f32[1664,128]{1,0:T(8,128)}, f32[1664,128]{1,0:T(8,128)S(1)}, u32[]{:S(2)}, u32[]{:S(2)}) collective-permute-start(f32[1664,128]{1,0:T(8,128)} %get-tuple-element.37.refs_0_), channel_id=1, source_target_pairs={{0,4},{1,5},{2,6},{3,7},{4,0},{5,1},{6,2},{7,3},{8,12},{9,13},{10,... | collective-permute-start | bytes 2555912 | tf_op jit(solution)/shard_map/ppermute | solution.py:343
  61.3 87.5 %collective-permute-start.9 = (f32[1664,128]{1,0:T(8,128)}, f32[1664,128]{1,0:T(8,128)S(1)}, u32[]{:S(2)}, u32[]{:S(2)}) collective-permute-start(f32[1664,128]{1,0:T(8,128)} %get-tuple-element.37.refs_0_), channel_id=1, source_target_pairs={{0,3},{1,2},{2,1},{3,0},{4,7},{5,6},{6,5},{7,4},{8,11},{9,10},{10,... | collective-permute-start | bytes 2555912 | tf_op jit(solution)/shard_map/ppermute | solution.py:343
  76.8 71.9 %copy-start.2 = (f32[1664,128]{1,0:T(8,128)}, f32[1664,128]{1,0:T(8,128)S(1)}, u32[]{:S(2)}) copy-start(f32[1664,128]{1,0:T(8,128)S(1)} %collective-permute-done.13.refs_7_) | copy-start | bytes 2555908
  76.8 72.0 %collective-permute-start.8 = (f32[1664,128]{1,0:T(8,128)}, f32[1664,128]{1,0:T(8,128)S(1)}, u32[]{:S(2)}, u32[]{:S(2)}) collective-permute-start(f32[1664,128]{1,0:T(8,128)} %get-tuple-element.37.refs_0_), channel_id=1, source_target_pairs={{0,2},{1,3},{2,0},{3,1},{4,6},{5,7},{6,4},{7,5},{8,10},{9,11},{10,... | collective-permute-start | bytes 2555912 | tf_op jit(solution)/shard_map/ppermute | solution.py:343
  95.4 53.4 %copy-start.3 = (f32[1664,128]{1,0:T(8,128)}, f32[1664,128]{1,0:T(8,128)S(1)}, u32[]{:S(2)}) copy-start(f32[1664,128]{1,0:T(8,128)S(1)} %collective-permute-done.12.refs_6_) | copy-start | bytes 2555908
  95.4 53.4 %collective-permute-start.7 = (f32[1664,128]{1,0:T(8,128)}, f32[1664,128]{1,0:T(8,128)S(1)}, u32[]{:S(2)}, u32[]{:S(2)}) collective-permute-start(f32[1664,128]{1,0:T(8,128)} %get-tuple-element.37.refs_0_), channel_id=1, source_target_pairs={{0,1},{1,0},{2,3},{3,2},{4,5},{5,4},{6,7},{7,6},{8,9},{9,8},{10,11... | collective-permute-start | bytes 2555912 | tf_op jit(solution)/shard_map/ppermute | solution.py:343
  148.7 0.9 copy-start.4
  148.8 1.2 copy-start.5
  148.8 1.5 copy-start.6
  148.8 1.8 copy-start.7
  148.8 2.0 copy-start.8
  175.1 9.7 %collective-permute-start.14 = (f32[1032,1024]{1,0:T(8,128)}, f32[1032,1024]{1,0:T(8,128)S(1)}, u32[]{:S(2)}, u32[]{:S(2)}) collective-permute-start(f32[1032,1024]{1,0:T(8,128)} %get-tuple-element.39.own), channel_id=1, source_target_pairs={{0,8},{8,0},{16,24},{24,16},{32,40},{40,32},{48,56},{56,48},{64,72... | collective-permute-start | bytes 12681224 | tf_op jit(solution)/shard_map/ppermute | solution.py:413
  184.8 2.0 copy-start.1
